TPU v7x, 512 devices: a whole 4x8x8 slice. The times are simulated.
512 devices in a mesh: wide: 128 (over y, z, core), rep: 4 (over x).
Axes of the slice: x: 4, y: 8, z: 8, core: 2. Of those that a mesh axis runs over, the one named last changes fastest.
Arguments:
- node_feats: bfloat16 [131072, 512], P('wide'), may hold values from -6 to 6
- w_self: bfloat16 [512, 512], replicated, may hold values from -0.25 to 0.25
- w_neigh: bfloat16 [512, 512], replicated, may hold values from -0.25 to 0.25
- send_rows: int32 [128, 128, 32], P('wide', None, 'rep'), may hold values from 0 to 1023
- tile_dst: int32 [128, 4, 128], P('wide', 'rep'), may hold values from 0 to 15
- tile_src: int32 [128, 4, 128], P('wide', 'rep'), may hold values from 0 to 31
- tile_bits: int32 [128, 4, 32768], P('wide', 'rep'), may hold values from 0 to 65280
- norm_count: int32 [131072], P('wide'), may hold values from 512 to 2048
- grad_out: bfloat16 [131072, 512], P(('wide', 'rep')), may hold values from -6 to 6
Outputs:
- out_feats: bfloat16 [131072, 512], P(('wide', 'rep'))
- grad_feats: bfloat16 [131072, 512], P(('wide', 'rep'))
- grad_self: bfloat16 [512, 512], replicated
- grad_neigh: bfloat16 [512, 512], replicated
All inputs are finite; a program needn't handle non-finite values.
Results may differ from a plain program's by a relative error of at most 0.014.
Values may be sent and summed in bfloat16 or wider, within the bound.
No kernel may reach another device: no remote copies, remote signals or barrier semaphores. Data moves between devices by JAX's collectives and lax.ppermute only.
A program may use at most 64 MiB of HBM per device.

v0:
```python
import math
import jax
import jax.numpy as jnp
from jax import lax
from jax.sharding import PartitionSpec as P

BLOCK = 64


def unpack_bits(packed, tile_count, block_size):
    shaped = packed.reshape(tile_count, block_size, block_size // 16)
    shift_list = jnp.arange(16, dtype=jnp.int32)
    bit_grid = jnp.bitwise_and(jnp.right_shift(shaped[..., None], shift_list), 1)
    return bit_grid.reshape(tile_count, block_size, block_size)


def times_transposed(left, right):
    return lax.dot_general(
        left, right, (((1,), (1,)), ((), ())), preferred_element_type=jnp.float32
    )


def on_device(
    node_feats, w_self, w_neigh, send_rows, tile_dst, tile_src, tile_bits, norm_count, grad_out
):
    node_rows, feat_width = node_feats.shape
    peer_count = lax.axis_size("wide")
    replicas = lax.axis_size("rep")
    slot_count = send_rows.shape[2]
    tile_total = tile_dst.shape[2]
    block_size = BLOCK
    quarter = node_rows // replicas
    rep_index = lax.axis_index("rep")
    dst_count = node_rows // block_size
    group_size = math.gcd(tile_total, 32)
    send_index = send_rows[0]
    outgoing = jnp.take(node_feats, send_index.reshape(-1), axis=0).reshape(
        peer_count, slot_count, feat_width
    )
    incoming = lax.all_to_all(outgoing, "wide", split_axis=0, concat_axis=0, tiled=True)
    src_table = jnp.concatenate(
        [node_feats, incoming.reshape(peer_count * slot_count, feat_width)], axis=0
    )
    source_blocks = src_table.reshape(-1, block_size, feat_width)
    src_count = source_blocks.shape[0]
    tile_masks = unpack_bits(tile_bits[0, 0], tile_total, block_size).astype(jnp.bfloat16)
    grouped_masks = tile_masks.reshape(-1, group_size, block_size, block_size)
    grouped_dst = tile_dst[0, 0].reshape(-1, group_size)
    grouped_src = tile_src[0, 0].reshape(-1, group_size)

    def forward_group(running, group_items):
        mask_part, dst_part, src_part = group_items
        picked = jnp.take(source_blocks, src_part, axis=0)
        products = jnp.einsum("tij,tjf->tif", mask_part, picked, preferred_element_type=jnp.float32)
        return (running.at[dst_part].add(products), None)

    partial_sum, _ = lax.scan(
        forward_group,
        jnp.zeros((dst_count, block_size, feat_width), jnp.float32),
        (grouped_masks, grouped_dst, grouped_src),
    )
    partial_sum = partial_sum.reshape(node_rows, feat_width)
    summed = lax.psum(partial_sum, "rep")
    own_sums = lax.dynamic_slice_in_dim(summed, rep_index * quarter, quarter, 0)
    scale_all = lax.rsqrt(norm_count.astype(jnp.float32))
    own_scale = lax.dynamic_slice_in_dim(scale_all, rep_index * quarter, quarter, 0)
    own_feats = lax.dynamic_slice_in_dim(node_feats, rep_index * quarter, quarter, 0)
    own_agg = (own_sums * own_scale[:, None]).astype(jnp.bfloat16)
    pre_act = jnp.dot(own_feats, w_self, preferred_element_type=jnp.float32) + jnp.dot(
        own_agg, w_neigh, preferred_element_type=jnp.float32
    )
    sigmoid = jax.nn.sigmoid(pre_act)
    out_feats = (pre_act * sigmoid).astype(jnp.bfloat16)
    grad_pre = (grad_out.astype(jnp.float32) * sigmoid * (1.0 + pre_act * (1.0 - sigmoid))).astype(
        jnp.bfloat16
    )
    dims_rows = (((0,), (0,)), ((), ()))
    self_term = lax.dot_general(own_feats, grad_pre, dims_rows, preferred_element_type=jnp.float32)
    neigh_term = lax.dot_general(own_agg, grad_pre, dims_rows, preferred_element_type=jnp.float32)
    summed_self, summed_neigh = lax.psum((self_term, neigh_term), ("wide", "rep"))
    own_grad_agg = (times_transposed(grad_pre, w_neigh) * own_scale[:, None]).astype(jnp.bfloat16)
    grad_agg = lax.all_gather(own_grad_agg, "rep", axis=0, tiled=True)
    agg_blocks = grad_agg.reshape(dst_count, block_size, feat_width)

    def backward_group(running, group_items):
        mask_part, dst_part, src_part = group_items
        picked = jnp.take(agg_blocks, dst_part, axis=0)
        products = jnp.einsum("tij,tif->tjf", mask_part, picked, preferred_element_type=jnp.float32)
        return (running.at[src_part].add(products), None)

    table_grad, _ = lax.scan(
        backward_group,
        jnp.zeros((src_count, block_size, feat_width), jnp.float32),
        (grouped_masks, grouped_dst, grouped_src),
    )
    table_grad = table_grad.reshape(src_count * block_size, feat_width)
    local_grad = table_grad[:node_rows]
    halo_grad = (
        table_grad[node_rows:].astype(jnp.bfloat16).reshape(peer_count, slot_count, feat_width)
    )
    returned = lax.all_to_all(halo_grad, "wide", split_axis=0, concat_axis=0, tiled=True)
    returned_rows = (
        jnp.zeros((node_rows, feat_width), jnp.float32)
        .at[send_index.reshape(-1)]
        .add(returned.reshape(-1, feat_width).astype(jnp.float32))
    )
    own_total = lax.psum_scatter(
        (local_grad + returned_rows).astype(jnp.bfloat16), "rep", scatter_dimension=0, tiled=True
    ).astype(jnp.float32)
    grad_feats = (own_total + times_transposed(grad_pre, w_self)).astype(jnp.bfloat16)
    return (
        out_feats,
        grad_feats,
        summed_self.astype(jnp.bfloat16),
        summed_neigh.astype(jnp.bfloat16),
    )


def solution(mesh):
    in_specs = (
        P("wide", None),
        P(),
        P(),
        P("wide", None, "rep"),
        P("wide", "rep", None),
        P("wide", "rep", None),
        P("wide", "rep", None),
        P("wide"),
        P(("wide", "rep"), None),
    )
    out_specs = (P(("wide", "rep"), None), P(("wide", "rep"), None), P(), P())
    return jax.shard_map(
        on_device, mesh=mesh, in_specs=in_specs, out_specs=out_specs, check_vma=False
    )
```

profile of v0, /device:TPU:1, one launch (start us, length us, event | category | flops | bytes accessed | tf_op | source)
XLA Modules:
  0.0 459.9 jit_solution(16109861953868291241)
XLA Ops:
  7.2 0.8 compare_and_fusion.2
  7.9 0.8 copy.18
  8.7 0.1 copy.17
  8.8 0.1 reshape_squeeze.15
  9.0 5.4 %gather_fusion.2 = bf16[1024,512]{1,0:T(8,128)(2,1)S(1)} fusion(bf16[1024,512]{1,0:T(8,128)(2,1)} %param.13, s32[1024]{0:T(1024)S(1)} %broadcast_clamp_fusion), kind=kCustom, calls=%fused_computation.2 | custom fusion | bytes 2101248 | tf_op jit(solution)/shard_map/jit(_take)/gather | solution.py:37
  14.4 1.2 bitcast_select_fusion
  15.5 18.4 %all-to-all-start = ((bf16[128,8,512]{2,1,0:T(8,128)(2,1)}), bf16[128,8,512]{2,1,0:T(8,128)(2,1)S(1)}, u32[]{:S(2)}, u32[]{:S(2)}) async-start(bf16[128,8,512]{2,1,0:T(8,128)(2,1)} %bitcast_select_fusion), calls=%async_computation | async-start | bytes 2097152 | tf_op jit(solution)/shard_map/all_to_all | solution.py:40
  34.0 0.5 broadcast.165
  34.5 0.7 reduce.9
  35.2 0.7 reduce.11
  35.9 0.1 reshape_squeeze.13
  36.0 0.1 shift_right_arithmetic.27
  36.1 1.0 reduce.10
  37.1 5.7 %shift_right_arithmetic.23 = s32[128,64,4]{2,1,0:T(8,128)} reshape(s32[32768]{0:T(1024)S(1)} %reduce.10) | data formatting | bytes 262144 | tf_op jit(solution)/shard_map/shift_right_arithmetic | solution.py:13
  42.7 3.0 copy.16
  45.7 0.3 shift_right_arithmetic.24
  46.1 2.1 and_convert_fusion
  48.2 16.2 %all-to-all-done = bf16[128,8,512]{2,1,0:T(8,128)(2,1)S(1)} async-done(((bf16[128,8,512]{2,1,0:T(8,128)(2,1)}), bf16[128,8,512]{2,1,0:T(8,128)(2,1)S(1)}, u32[]{:S(2)}, u32[]{:S(2)}) %all-to-all-start) | async-done | bytes 1048608 | tf_op jit(solution)/shard_map/all_to_all | solution.py:40
  64.4 1.5 pad_maximum_fusion
  65.9 0.2 broadcast_in_dim.43
  66.1 58.5 %while.20 = (s32[]{:T(128)}, f32[16,64,512]{2,1,0:T(8,128)S(1)}, s32[4,32]{1,0:T(4,128)S(1)}, bf16[4,32,64,64]{2,3,1,0:T(8,128)(2,1)}, s32[4,32]{1,0:T(4,128)S(1)}, /*index=5*/bf16[32,64,512]{2,1,0:T(8,128)(2,1)}, s32[]{:T(128)}) while((s32[]{:T(128)}, f32[16,64,512]{2,1,0:T(8,128)S(1)}, s32[4,32]{1,0:T(4,128)S(1)}, ...), condition=%wide.region_2.3_spmd, body=%wide.region_0.0_spmd.sunk | while | flops 136316288 | bytes 23598240 | solution.py:57
  66.2 3.6 gather_fusion
  69.8 4.5 fusion.53
  74.3 6.5 %scatter_fusion = f32[16,64,512]{2,1,0:T(8,128)S(1)} fusion(f32[16,64,512]{2,1,0:T(8,128)S(1)} %get-tuple-element.204, s32[32]{0:T(128)S(1)} %get-tuple-element.186, f32[32,64,512]{2,1,0:T(8,128)} %fusion.53), kind=kCustom, calls=%fused_computation.3.clone.1 | custom fusion | flops 1048576 | bytes 12583040 | tf_op jit(solution)/shard_map/while/body/eval_jaxpr/scatter-add | solution.py:55
  80.8 3.6 gather_fusion
  84.4 4.5 fusion.53
  88.9 6.5 %scatter_fusion = f32[16,64,512]{2,1,0:T(8,128)S(1)} fusion(f32[16,64,512]{2,1,0:T(8,128)S(1)} %get-tuple-element.204, s32[32]{0:T(128)S(1)} %get-tuple-element.186, f32[32,64,512]{2,1,0:T(8,128)} %fusion.53), kind=kCustom, calls=%fused_computation.3.clone.1 | custom fusion | flops 1048576 | bytes 12583040 | tf_op jit(solution)/shard_map/while/body/eval_jaxpr/scatter-add | solution.py:55
  95.4 3.6 gather_fusion
  99.1 4.5 fusion.53
  103.5 6.5 %scatter_fusion = f32[16,64,512]{2,1,0:T(8,128)S(1)} fusion(f32[16,64,512]{2,1,0:T(8,128)S(1)} %get-tuple-element.204, s32[32]{0:T(128)S(1)} %get-tuple-element.186, f32[32,64,512]{2,1,0:T(8,128)} %fusion.53), kind=kCustom, calls=%fused_computation.3.clone.1 | custom fusion | flops 1048576 | bytes 12583040 | tf_op jit(solution)/shard_map/while/body/eval_jaxpr/scatter-add | solution.py:55
  110.1 3.6 gather_fusion
  113.7 4.5 fusion.53
  118.2 6.5 %scatter_fusion = f32[16,64,512]{2,1,0:T(8,128)S(1)} fusion(f32[16,64,512]{2,1,0:T(8,128)S(1)} %get-tuple-element.204, s32[32]{0:T(128)S(1)} %get-tuple-element.186, f32[32,64,512]{2,1,0:T(8,128)} %fusion.53), kind=kCustom, calls=%fused_computation.3.clone.1 | custom fusion | flops 1048576 | bytes 12583040 | tf_op jit(solution)/shard_map/while/body/eval_jaxpr/scatter-add | solution.py:55
  124.7 1.3 copy-done.1
  126.0 0.2 all-gather.2.cloned.1.call-start
  126.4 1.2 fusion.29
  127.6 62.0 %all-reduce.4.cloned.1.call-done = f32[1024,512]{1,0:T(8,128)} async-done(((f32[1024,512]{1,0:T(8,128)}), f32[1024,512]{1,0:T(8,128)}) %all-reduce.4.cloned.1.call-update) | async-done | bytes 2097168 | tf_op jit(solution)/shard_map/psum | solution.py:63
  189.6 2.3 multiply_convert_fusion
  192.0 1.0 fusion.24
  193.0 28.4 %all-gather.2.cloned.1.call-done = bf16[1024,512]{1,0:T(8,128)(2,1)} async-done(((bf16[256,512]{1,0:T(8,128)(2,1)}), bf16[1024,512]{1,0:T(8,128)(2,1)}) %all-gather.2.cloned.1.call-update) | async-done | bytes 1048592 | tf_op jit(solution)/shard_map/all_gather | solution.py:82
  221.4 2.5 broadcast_in_dim.46
  223.9 62.5 %while.21 = (s32[]{:T(128)}, f32[32,64,512]{2,1,0:T(8,128)}, s32[4,32]{1,0:T(4,128)S(1)}, bf16[4,32,64,64]{2,3,1,0:T(8,128)(2,1)}, s32[4,32]{1,0:T(4,128)S(1)}, /*index=5*/bf16[16,64,512]{2,1,0:T(8,128)(2,1)}, s32[]{:T(128)}) while((s32[]{:T(128)}, f32[32,64,512]{2,1,0:T(8,128)}, s32[4,32]{1,0:T(4,128)S(1)}, ...), condition=%wide.region_6.7_spmd, body=%wide.region_4.6_spmd.sunk | while | flops 136316288 | bytes 23598240 | solution.py:91
  224.0 1.9 gather_fusion.1
  225.9 3.8 fusion.57
  229.7 9.8 %scatter_fusion.1 = f32[32,64,512]{2,1,0:T(8,128)} fusion(f32[32,64,512]{2,1,0:T(8,128)} %get-tuple-element.225, s32[32]{0:T(128)S(1)} %get-tuple-element.194, f32[32,64,512]{2,1,0:T(8,128)} %fusion.57), kind=kCustom, calls=%fused_computation.4.clone.1 | custom fusion | flops 1048576 | bytes 12583040 | tf_op jit(solution)/shard_map/while/body/eval_jaxpr/scatter-add | solution.py:89
  239.5 1.9 gather_fusion.1
  241.4 3.7 fusion.57
  245.1 9.8 %scatter_fusion.1 = f32[32,64,512]{2,1,0:T(8,128)} fusion(f32[32,64,512]{2,1,0:T(8,128)} %get-tuple-element.225, s32[32]{0:T(128)S(1)} %get-tuple-element.194, f32[32,64,512]{2,1,0:T(8,128)} %fusion.57), kind=kCustom, calls=%fused_computation.4.clone.1 | custom fusion | flops 1048576 | bytes 12583040 | tf_op jit(solution)/shard_map/while/body/eval_jaxpr/scatter-add | solution.py:89
  255.0 1.9 gather_fusion.1
  256.9 3.7 fusion.57
  260.6 10.0 %scatter_fusion.1 = f32[32,64,512]{2,1,0:T(8,128)} fusion(f32[32,64,512]{2,1,0:T(8,128)} %get-tuple-element.225, s32[32]{0:T(128)S(1)} %get-tuple-element.194, f32[32,64,512]{2,1,0:T(8,128)} %fusion.57), kind=kCustom, calls=%fused_computation.4.clone.1 | custom fusion | flops 1048576 | bytes 12583040 | tf_op jit(solution)/shard_map/while/body/eval_jaxpr/scatter-add | solution.py:89
  270.7 1.9 gather_fusion.1
  272.6 3.7 fusion.57
  276.3 10.1 %scatter_fusion.1 = f32[32,64,512]{2,1,0:T(8,128)} fusion(f32[32,64,512]{2,1,0:T(8,128)} %get-tuple-element.225, s32[32]{0:T(128)S(1)} %get-tuple-element.194, f32[32,64,512]{2,1,0:T(8,128)} %fusion.57), kind=kCustom, calls=%fused_computation.4.clone.1 | custom fusion | flops 1048576 | bytes 12583040 | tf_op jit(solution)/shard_map/while/body/eval_jaxpr/scatter-add | solution.py:89
  286.4 2.8 slice.22
  289.2 15.9 %all-to-all-start.1 = ((bf16[128,8,512]{2,1,0:T(8,128)(2,1)}), bf16[128,8,512]{2,1,0:T(8,128)(2,1)}, u32[]{:S(2)}, u32[]{:S(2)}) async-start(bf16[128,8,512]{2,1,0:T(8,128)(2,1)} %bitcast.21), calls=%async_computation.1 | async-start | bytes 2097152 | tf_op jit(solution)/shard_map/all_to_all | solution.py:101
  305.1 1.9 slice.11
  307.0 28.2 %all-to-all-done.1 = bf16[128,8,512]{2,1,0:T(8,128)(2,1)} async-done(((bf16[128,8,512]{2,1,0:T(8,128)(2,1)}), bf16[128,8,512]{2,1,0:T(8,128)(2,1)}, u32[]{:S(2)}, u32[]{:S(2)}) %all-to-all-start.1) | async-done | bytes 1048608 | tf_op jit(solution)/shard_map/all_to_all | solution.py:101
  335.2 8.0 %scatter_custom_fusion.2 = f32[1024,512]{1,0:T(8,128)S(1)} fusion(f32[1024,512]{1,0:T(8,128)S(1)} %bitcast.83, s32[1024]{0:T(1024)S(1)} %bitcast.86, bf16[128,8,512]{2,1,0:T(8,128)(2,1)} %all-to-all-done.1), kind=kCustom, calls=%fused_computation.45 | custom fusion | flops 1048576 | bytes 3145728 | tf_op jit(solution)/shard_map/scatter-add | solution.py:105
  343.2 1.1 convert_element_type.58
  344.3 1.5 fusion.33
  345.8 1.3 fusion.27
  347.0 104.4 %all-reduce.5 = (bf16[512,512]{1,0:T(8,128)(2,1)}, bf16[512,512]{1,0:T(8,128)(2,1)}) all-reduce(f32[512,512]{1,0:T(8,128)S(1)} %fusion.27, f32[512,512]{1,0:T(8,128)S(1)} %fusion.33), channel_id=1, replica_groups=mesh['wide'=128,'rep'=4] {'wide','rep'}, use_global_device_ids=true, to_apply=%region_9.10 | all-reduce | flops 524288 | bytes 3145728 | tf_op jit(solution)/shard_map/psum | solution.py:80
  451.4 2.0 fusion.25
  (51 shorter events, 0.6 us)
Async XLA Ops:
  7.2 182.5 %copy-start = (bf16[512,512]{1,0:T(8,128)(2,1)S(1)}, bf16[512,512]{1,0:T(8,128)(2,1)}, u32[]{:S(2)}) copy-start(bf16[512,512]{1,0:T(8,128)(2,1)} %param.15) | copy-start | bytes 1572868
  14.3 20.2 %copy-start.6 = (s32[1,1,128]{2,1,0:T(1,128)S(1)}, s32[1,1,128]{2,1,0:T(1,128)}, u32[]{:S(2)}) copy-start(s32[1,1,128]{2,1,0:T(1,128)} %param.17) | copy-start | bytes 1540
  14.3 20.9 %copy-start.7 = (s32[1,1,128]{2,1,0:T(1,128)S(1)}, s32[1,1,128]{2,1,0:T(1,128)}, u32[]{:S(2)}) copy-start(s32[1,1,128]{2,1,0:T(1,128)} %param.18) | copy-start | bytes 1540
  14.4 21.8 %copy-start.4 = (s32[1,1,32768]{2,1,0:T(1,128)S(1)}, s32[1,1,32768]{2,1,0:T(1,128)}, u32[]{:S(2)}) copy-start(s32[1,1,32768]{2,1,0:T(1,128)} %param.19) | copy-start | bytes 393220
  15.5 48.9 %all-to-all-start = ((bf16[128,8,512]{2,1,0:T(8,128)(2,1)}), bf16[128,8,512]{2,1,0:T(8,128)(2,1)S(1)}, u32[]{:S(2)}, u32[]{:S(2)}) async-start(bf16[128,8,512]{2,1,0:T(8,128)(2,1)} %bitcast_select_fusion), calls=%async_computation | async-start | bytes 2097152 | tf_op jit(solution)/shard_map/all_to_all | solution.py:40
  34.0 155.7 %all-reduce.4.cloned.1.call-start = ((), (), s32[]{:S(2)}) async-start(), calls=%async_computation.3 | async-start | bytes 4194304 | tf_op jit(solution)/shard_map/psum | solution.py:63
  46.1 18.3 %copy-start.2 = (bf16[1024,512]{1,0:T(8,128)(2,1)S(1)}, bf16[1024,512]{1,0:T(8,128)(2,1)}, u32[]{:S(2)}) copy-start(bf16[1024,512]{1,0:T(8,128)(2,1)} %param.13) | copy-start | bytes 3145732
  124.7 1.3 copy-start.1
  124.7 1.6 copy-start.5
  124.7 1.7 copy-start.3
  126.0 95.4 %all-gather.2.cloned.1.call-start = ((), (), s32[]{:S(2)}) async-start(), calls=%async_computation.4 | async-start | bytes 1310720 | tf_op jit(solution)/shard_map/all_gather | solution.py:82
  289.2 46.0 %all-to-all-start.1 = ((bf16[128,8,512]{2,1,0:T(8,128)(2,1)}), bf16[128,8,512]{2,1,0:T(8,128)(2,1)}, u32[]{:S(2)}, u32[]{:S(2)}) async-start(bf16[128,8,512]{2,1,0:T(8,128)(2,1)} %bitcast.21), calls=%async_computation.1 | async-start | bytes 2097152 | tf_op jit(solution)/shard_map/all_to_all | solution.py:101
  305.1 146.3 %reduce-scatter.2.cloned.1.call-start = ((), (), s32[]{:S(2)}) async-start(), calls=%async_computation.5 | async-start | bytes 1310720 | tf_op jit(solution)/shard_map/reduce_scatter | solution.py:107
Sparse Core Ops, SparseCore 0:
  126.2 63.4 all-reduce.3
  193.2 28.2 all-gather.1
  344.4 20.2 reduce-scatter.1
where the time goes:
time: 462 us; the launch traced here: 460 us
  waiting for transfers between devices  135 us (29%)
  blocking collectives  104 us (23%)
  other arithmetic  82.7 us (18%)
  local copies, waits for them, and re-layouts  47 us (10%)
  matrix products  42.2 us (9%)
  starting transfers between devices  34.6 us (7%)
  between operations  14 us (3%)
    psum x1, blocking collectives, on_device(): lax.psum((self_term, neigh_term), ('wide', 'rep'))  104 us
    psum x1, waiting for transfers between devices, on_device(): summed = lax.psum(partial_sum, 'rep')  62 us
    scatter-add x4, other arithmetic, backward_group(): return (running.at[src_part].add(products), None)  39.6 us
    all_gather x1, waiting for transfers between devices, on_device(): grad_agg = lax.all_gather(own_grad_agg, 'rep', axis=0, tiled=True)  28.4 us
    all_to_all x1, waiting for transfers between devices, on_device(): lax.all_to_all(halo_grad, 'wide', split_axis=0, concat_axis=0, tiled=True)  28.2 us
    scatter-add x4, other arithmetic, forward_group(): return (running.at[dst_part].add(products), None)  25.9 us
    all_to_all x1, starting transfers between devices, on_device(): lax.all_to_all(outgoing, 'wide', split_axis=0, concat_axis=0, tiled=True)  18.4 us
    dot_general x4, matrix products, forward_group(): jnp.einsum('tij,tjf->tif', mask_part, picked, preferred_element_type=jnp....  17.9 us
  transfers between devices with their start and end apart: 5, of which 4 were waited for; matrix products, arithmetic and copies ran while one was open for 4% of the time, Pallas kernels for 0%

commit v1 on v0

--- a/solution.py
+++ b/solution.py
@@ -77,7 +77,9 @@
     dims_rows = (((0,), (0,)), ((), ()))
     self_term = lax.dot_general(own_feats, grad_pre, dims_rows, preferred_element_type=jnp.float32)
     neigh_term = lax.dot_general(own_agg, grad_pre, dims_rows, preferred_element_type=jnp.float32)
-    summed_self, summed_neigh = lax.psum((self_term, neigh_term), ("wide", "rep"))
+    summed_self, summed_neigh = lax.psum(
+        lax.psum((self_term, neigh_term), axis_name="wide"), axis_name="rep"
+    )
     own_grad_agg = (times_transposed(grad_pre, w_neigh) * own_scale[:, None]).astype(jnp.bfloat16)
     grad_agg = lax.all_gather(own_grad_agg, "rep", axis=0, tiled=True)
     agg_blocks = grad_agg.reshape(dst_count, block_size, feat_width)

time: 462 us -> 575 us (1.24)
  waiting for transfers between devices: 135 us -> 298 us
  blocking collectives: 104 us -> 46.9 us
    psum x0 -> x1, waiting for transfers between devices: none -> 168 us  [on_device(): lax.psum((self_term, neigh_term), axis_name='wide')]
    psum x1, blocking collectives: 104 us -> 46.9 us  [on_device(): lax.psum(lax.psum((self_term, neigh_term), axis_name='wide'), axis_name='...]
  transfers between devices with their start and end apart: 5 -> 6, of which waited for: 4 -> 5; matrix products, arithmetic and copies ran while one was open for 4% -> 5% of each run, Pallas kernels for 0% -> 0%
where the time goes in v1:
time: 575 us; the launch traced here: 568 us
  waiting for transfers between devices  298 us (52%)
  other arithmetic  82.7 us (14%)
  local copies, waits for them, and re-layouts  47 us (8%)
  blocking collectives  46.9 us (8%)
  matrix products  44.2 us (8%)
  starting transfers between devices  34.6 us (6%)
  between operations  14 us (2%)
    psum x1, waiting for transfers between devices, on_device(): lax.psum((self_term, neigh_term), axis_name='wide')  168 us
    psum x1, waiting for transfers between devices, on_device(): summed = lax.psum(partial_sum, 'rep')  62 us
    psum x1, blocking collectives, on_device(): lax.psum(lax.psum((self_term, neigh_term), axis_name='wide'), axis_name='...  46.9 us
    scatter-add x4, other arithmetic, backward_group(): return (running.at[src_part].add(products), None)  39.6 us
    all_gather x1, waiting for transfers between devices, on_device(): grad_agg = lax.all_gather(own_grad_agg, 'rep', axis=0, tiled=True)  28.4 us
    scatter-add x4, other arithmetic, forward_group(): return (running.at[dst_part].add(products), None)  25.9 us
    all_to_all x1, waiting for transfers between devices, on_device(): lax.all_to_all(halo_grad, 'wide', split_axis=0, concat_axis=0, tiled=True)  23.6 us
    all_to_all x1, starting transfers between devices, on_device(): lax.all_to_all(outgoing, 'wide', split_axis=0, concat_axis=0, tiled=True)  18.4 us
  transfers between devices with their start and end apart: 6, of which 5 were waited for; matrix products, arithmetic and copies ran while one was open for 5% of the time, Pallas kernels for 0%

profile of v1, /device:TPU:1, one launch (start us, length us, event | category | flops | bytes accessed | tf_op | source)
XLA Modules:
  0.0 567.5 jit_solution(10825546299449742621)
XLA Ops:
  7.2 0.8 compare_and_fusion.2
  7.9 0.8 copy.18
  8.7 0.1 copy.17
  8.8 0.1 reshape_squeeze.15
  9.0 5.4 gather_fusion.2
  14.4 1.2 bitcast_select_fusion
  15.6 18.4 %all-to-all-start = ((bf16[128,8,512]{2,1,0:T(8,128)(2,1)}), bf16[128,8,512]{2,1,0:T(8,128)(2,1)S(1)}, u32[]{:S(2)}, u32[]{:S(2)}) async-start(bf16[128,8,512]{2,1,0:T(8,128)(2,1)} %bitcast_select_fusion), calls=%async_computation | async-start | bytes 2097152 | tf_op jit(solution)/shard_map/all_to_all | solution.py:40
  34.0 0.5 broadcast.165
  34.5 0.7 reduce.9
  35.2 0.7 reduce.11
  36.1 0.1 shift_right_arithmetic.27
  36.1 1.0 reduce.10
  37.1 5.7 shift_right_arithmetic.23
  42.8 3.0 copy.16
  45.8 0.3 shift_right_arithmetic.24
  46.1 2.1 and_convert_fusion
  48.3 16.2 %all-to-all-done = bf16[128,8,512]{2,1,0:T(8,128)(2,1)S(1)} async-done(((bf16[128,8,512]{2,1,0:T(8,128)(2,1)}), bf16[128,8,512]{2,1,0:T(8,128)(2,1)S(1)}, u32[]{:S(2)}, u32[]{:S(2)}) %all-to-all-start) | async-done | bytes 1048608 | tf_op jit(solution)/shard_map/all_to_all | solution.py:40
  64.4 1.5 pad_maximum_fusion
  65.9 0.2 broadcast_in_dim.43
  66.1 58.6 %while.20 = (s32[]{:T(128)}, f32[16,64,512]{2,1,0:T(8,128)S(1)}, s32[4,32]{1,0:T(4,128)S(1)}, bf16[4,32,64,64]{2,3,1,0:T(8,128)(2,1)}, s32[4,32]{1,0:T(4,128)S(1)}, /*index=5*/bf16[32,64,512]{2,1,0:T(8,128)(2,1)}, s32[]{:T(128)}) while((s32[]{:T(128)}, f32[16,64,512]{2,1,0:T(8,128)S(1)}, s32[4,32]{1,0:T(4,128)S(1)}, ...), condition=%wide.region_2.3_spmd, body=%wide.region_0.0_spmd.sunk | while | flops 136316288 | bytes 23598240 | solution.py:57
  66.2 3.6 gather_fusion
  69.8 4.5 fusion.53
  74.3 6.5 %scatter_fusion = f32[16,64,512]{2,1,0:T(8,128)S(1)} fusion(f32[16,64,512]{2,1,0:T(8,128)S(1)} %get-tuple-element.206, s32[32]{0:T(128)S(1)} %get-tuple-element.188, f32[32,64,512]{2,1,0:T(8,128)} %fusion.53), kind=kCustom, calls=%fused_computation.3.clone.1 | custom fusion | flops 1048576 | bytes 12583040 | tf_op jit(solution)/shard_map/while/body/eval_jaxpr/scatter-add | solution.py:55
  80.8 3.6 gather_fusion
  84.4 4.5 fusion.53
  88.9 6.5 %scatter_fusion = f32[16,64,512]{2,1,0:T(8,128)S(1)} fusion(f32[16,64,512]{2,1,0:T(8,128)S(1)} %get-tuple-element.206, s32[32]{0:T(128)S(1)} %get-tuple-element.188, f32[32,64,512]{2,1,0:T(8,128)} %fusion.53), kind=kCustom, calls=%fused_computation.3.clone.1 | custom fusion | flops 1048576 | bytes 12583040 | tf_op jit(solution)/shard_map/while/body/eval_jaxpr/scatter-add | solution.py:55
  95.5 3.6 gather_fusion
  99.1 4.5 fusion.53
  103.5 6.5 %scatter_fusion = f32[16,64,512]{2,1,0:T(8,128)S(1)} fusion(f32[16,64,512]{2,1,0:T(8,128)S(1)} %get-tuple-element.206, s32[32]{0:T(128)S(1)} %get-tuple-element.188, f32[32,64,512]{2,1,0:T(8,128)} %fusion.53), kind=kCustom, calls=%fused_computation.3.clone.1 | custom fusion | flops 1048576 | bytes 12583040 | tf_op jit(solution)/shard_map/while/body/eval_jaxpr/scatter-add | solution.py:55
  110.1 3.6 gather_fusion
  113.7 4.5 fusion.53
  118.2 6.5 %scatter_fusion = f32[16,64,512]{2,1,0:T(8,128)S(1)} fusion(f32[16,64,512]{2,1,0:T(8,128)S(1)} %get-tuple-element.206, s32[32]{0:T(128)S(1)} %get-tuple-element.188, f32[32,64,512]{2,1,0:T(8,128)} %fusion.53), kind=kCustom, calls=%fused_computation.3.clone.1 | custom fusion | flops 1048576 | bytes 12583040 | tf_op jit(solution)/shard_map/while/body/eval_jaxpr/scatter-add | solution.py:55
  124.7 1.3 copy-done.1
  126.1 0.2 all-gather.2.cloned.1.call-start
  126.4 1.2 fusion.29
  127.6 62.0 %all-reduce.6.cloned.1.call-done = f32[1024,512]{1,0:T(8,128)} async-done(((f32[1024,512]{1,0:T(8,128)}), f32[1024,512]{1,0:T(8,128)}) %all-reduce.6.cloned.1.call-update) | async-done | bytes 2097168 | tf_op jit(solution)/shard_map/psum | solution.py:63
  189.7 2.3 multiply_convert_fusion
  192.0 1.0 fusion.24
  193.1 28.4 %all-gather.2.cloned.1.call-done = bf16[1024,512]{1,0:T(8,128)(2,1)} async-done(((bf16[256,512]{1,0:T(8,128)(2,1)}), bf16[1024,512]{1,0:T(8,128)(2,1)}) %all-gather.2.cloned.1.call-update) | async-done | bytes 1048592 | tf_op jit(solution)/shard_map/all_gather | solution.py:84
  221.5 2.5 broadcast_in_dim.46
  224.0 62.4 %while.21 = (s32[]{:T(128)}, f32[32,64,512]{2,1,0:T(8,128)}, s32[4,32]{1,0:T(4,128)S(1)}, bf16[4,32,64,64]{2,3,1,0:T(8,128)(2,1)}, s32[4,32]{1,0:T(4,128)S(1)}, /*index=5*/bf16[16,64,512]{2,1,0:T(8,128)(2,1)}, s32[]{:T(128)}) while((s32[]{:T(128)}, f32[32,64,512]{2,1,0:T(8,128)}, s32[4,32]{1,0:T(4,128)S(1)}, ...), condition=%wide.region_6.7_spmd, body=%wide.region_4.6_spmd.sunk | while | flops 136316288 | bytes 23598240 | solution.py:93
  224.0 1.9 gather_fusion.1
  225.9 3.8 fusion.57
  229.7 9.7 %scatter_fusion.1 = f32[32,64,512]{2,1,0:T(8,128)} fusion(f32[32,64,512]{2,1,0:T(8,128)} %get-tuple-element.227, s32[32]{0:T(128)S(1)} %get-tuple-element.196, f32[32,64,512]{2,1,0:T(8,128)} %fusion.57), kind=kCustom, calls=%fused_computation.4.clone.1 | custom fusion | flops 1048576 | bytes 12583040 | tf_op jit(solution)/shard_map/while/body/eval_jaxpr/scatter-add | solution.py:91
  239.5 1.9 gather_fusion.1
  241.4 3.7 fusion.57
  245.1 9.9 %scatter_fusion.1 = f32[32,64,512]{2,1,0:T(8,128)} fusion(f32[32,64,512]{2,1,0:T(8,128)} %get-tuple-element.227, s32[32]{0:T(128)S(1)} %get-tuple-element.196, f32[32,64,512]{2,1,0:T(8,128)} %fusion.57), kind=kCustom, calls=%fused_computation.4.clone.1 | custom fusion | flops 1048576 | bytes 12583040 | tf_op jit(solution)/shard_map/while/body/eval_jaxpr/scatter-add | solution.py:91
  255.0 1.9 gather_fusion.1
  256.9 3.8 fusion.57
  260.7 9.9 %scatter_fusion.1 = f32[32,64,512]{2,1,0:T(8,128)} fusion(f32[32,64,512]{2,1,0:T(8,128)} %get-tuple-element.227, s32[32]{0:T(128)S(1)} %get-tuple-element.196, f32[32,64,512]{2,1,0:T(8,128)} %fusion.57), kind=kCustom, calls=%fused_computation.4.clone.1 | custom fusion | flops 1048576 | bytes 12583040 | tf_op jit(solution)/shard_map/while/body/eval_jaxpr/scatter-add | solution.py:91
  270.7 1.9 gather_fusion.1
  272.6 3.7 fusion.57
  276.3 10.0 %scatter_fusion.1 = f32[32,64,512]{2,1,0:T(8,128)} fusion(f32[32,64,512]{2,1,0:T(8,128)} %get-tuple-element.227, s32[32]{0:T(128)S(1)} %get-tuple-element.196, f32[32,64,512]{2,1,0:T(8,128)} %fusion.57), kind=kCustom, calls=%fused_computation.4.clone.1 | custom fusion | flops 1048576 | bytes 12583040 | tf_op jit(solution)/shard_map/while/body/eval_jaxpr/scatter-add | solution.py:91
  286.4 2.7 slice.22
  289.1 15.9 %all-to-all-start.1 = ((bf16[128,8,512]{2,1,0:T(8,128)(2,1)}), bf16[128,8,512]{2,1,0:T(8,128)(2,1)}, u32[]{:S(2)}, u32[]{:S(2)}) async-start(bf16[128,8,512]{2,1,0:T(8,128)(2,1)} %bitcast.21), calls=%async_computation.1 | async-start | bytes 2097152 | tf_op jit(solution)/shard_map/all_to_all | solution.py:103
  305.0 2.3 fusion.27
  307.3 2.4 fusion.33
  309.8 1.9 slice.11
  311.7 23.6 %all-to-all-done.1 = bf16[128,8,512]{2,1,0:T(8,128)(2,1)} async-done(((bf16[128,8,512]{2,1,0:T(8,128)(2,1)}), bf16[128,8,512]{2,1,0:T(8,128)(2,1)}, u32[]{:S(2)}, u32[]{:S(2)}) %all-to-all-start.1) | async-done | bytes 1048608 | tf_op jit(solution)/shard_map/all_to_all | solution.py:103
  335.3 8.0 %scatter_custom_fusion.2 = f32[1024,512]{1,0:T(8,128)S(1)} fusion(f32[1024,512]{1,0:T(8,128)S(1)} %bitcast.83, s32[1024]{0:T(1024)S(1)} %bitcast.86, bf16[128,8,512]{2,1,0:T(8,128)(2,1)} %all-to-all-done.1), kind=kCustom, calls=%fused_computation.45 | custom fusion | flops 1048576 | bytes 3145728 | tf_op jit(solution)/shard_map/scatter-add | solution.py:107
  343.2 1.1 convert_element_type.58
  344.4 167.7 %all-reduce.8.cloned.1.call-done = (f32[512,512]{1,0:T(8,128)}, f32[512,512]{1,0:T(8,128)}) async-done(((f32[512,512]{1,0:T(8,128)}, f32[512,512]{1,0:T(8,128)}), (f32[512,512]{1,0:T(8,128)}, f32[512,512]{1,0:T(8,128)})) %all-reduce.8.cloned.1.call-update) | async-done | bytes 2097168 | tf_op jit(solution)/shard_map/psum | solution.py:81
  512.1 46.9 %all-reduce.9 = (bf16[512,512]{1,0:T(8,128)(2,1)}, bf16[512,512]{1,0:T(8,128)(2,1)}) all-reduce(f32[512,512]{1,0:T(8,128)} %get-tuple-element.106, f32[512,512]{1,0:T(8,128)} %get-tuple-element.107), channel_id=1, replica_groups=mesh['wide'=128,'rep'=4] {'rep'}, use_global_device_ids=true, to_apply=%region_10.11 | all-reduce | flops 524288 | bytes 3145728 | tf_op jit(solution)/shard_map/psum | solution.py:80
  559.0 2.0 fusion.25
  (54 shorter events, 0.7 us)
Async XLA Ops:
  7.2 182.5 %copy-start = (bf16[512,512]{1,0:T(8,128)(2,1)S(1)}, bf16[512,512]{1,0:T(8,128)(2,1)}, u32[]{:S(2)}) copy-start(bf16[512,512]{1,0:T(8,128)(2,1)} %param.15) | copy-start | bytes 1572868
  14.3 20.2 %copy-start.6 = (s32[1,1,128]{2,1,0:T(1,128)S(1)}, s32[1,1,128]{2,1,0:T(1,128)}, u32[]{:S(2)}) copy-start(s32[1,1,128]{2,1,0:T(1,128)} %param.17) | copy-start | bytes 1540
  14.3 20.9 %copy-start.7 = (s32[1,1,128]{2,1,0:T(1,128)S(1)}, s32[1,1,128]{2,1,0:T(1,128)}, u32[]{:S(2)}) copy-start(s32[1,1,128]{2,1,0:T(1,128)} %param.18) | copy-start | bytes 1540
  14.4 21.8 %copy-start.4 = (s32[1,1,32768]{2,1,0:T(1,128)S(1)}, s32[1,1,32768]{2,1,0:T(1,128)}, u32[]{:S(2)}) copy-start(s32[1,1,32768]{2,1,0:T(1,128)} %param.19) | copy-start | bytes 393220
  15.6 48.9 %all-to-all-start = ((bf16[128,8,512]{2,1,0:T(8,128)(2,1)}), bf16[128,8,512]{2,1,0:T(8,128)(2,1)S(1)}, u32[]{:S(2)}, u32[]{:S(2)}) async-start(bf16[128,8,512]{2,1,0:T(8,128)(2,1)} %bitcast_select_fusion), calls=%async_computation | async-start | bytes 2097152 | tf_op jit(solution)/shard_map/all_to_all | solution.py:40
  34.0 155.7 %all-reduce.6.cloned.1.call-start = ((), (), s32[]{:S(2)}) async-start(), calls=%async_computation.3 | async-start | bytes 4194304 | tf_op jit(solution)/shard_map/psum | solution.py:63
  46.1 18.3 %copy-start.2 = (bf16[1024,512]{1,0:T(8,128)(2,1)S(1)}, bf16[1024,512]{1,0:T(8,128)(2,1)}, u32[]{:S(2)}) copy-start(bf16[1024,512]{1,0:T(8,128)(2,1)} %param.13) | copy-start | bytes 3145732
  124.7 1.3 copy-start.1
  124.7 1.6 copy-start.5
  124.7 1.7 copy-start.3
  126.1 95.4 %all-gather.2.cloned.1.call-start = ((), (), s32[]{:S(2)}) async-start(), calls=%async_computation.4 | async-start | bytes 1310720 | tf_op jit(solution)/shard_map/all_gather | solution.py:84
  289.1 46.2 %all-to-all-start.1 = ((bf16[128,8,512]{2,1,0:T(8,128)(2,1)}), bf16[128,8,512]{2,1,0:T(8,128)(2,1)}, u32[]{:S(2)}, u32[]{:S(2)}) async-start(bf16[128,8,512]{2,1,0:T(8,128)(2,1)} %bitcast.21), calls=%async_computation.1 | async-start | bytes 2097152 | tf_op jit(solution)/shard_map/all_to_all | solution.py:103
  304.9 207.2 %all-reduce.8.cloned.1.call-start = ((), (), s32[]{:S(2)}) async-start(), calls=%async_computation.6 | async-start | bytes 4194304 | tf_op jit(solution)/shard_map/psum | solution.py:81
  309.7 249.3 %reduce-scatter.2.cloned.1.call-start = ((), (), s32[]{:S(2)}) async-start(), calls=%async_computation.5 | async-start | bytes 1310720 | tf_op jit(solution)/shard_map/reduce_scatter | solution.py:109
Sparse Core Ops, SparseCore 0:
  126.2 63.4 all-reduce.5
  193.2 28.2 all-gather.1
  309.9 202.1 all-reduce.7
  515.0 30.7 reduce-scatter.1
